TPU v7x, 32 devices: a whole 2x2x4 slice. The times are simulated.
32 devices in a mesh: dp: 2 (over core), row: 4 (over y, x), col: 4 (over z).
Axes of the slice: x: 2, y: 2, z: 4, core: 2. Of those that a mesh axis runs over, the one named last changes fastest.
Arguments:
- inputs: bfloat16 [2, 16, 4, 16, 2048], P('dp', 'row', None, None, 'col'), may hold values from -6 to 6
- up_weight: bfloat16 [2048, 4096], P(None, 'col'), may hold values from -0.1875 to 0.1875
- down_weight: bfloat16 [2048, 4096], P(None, 'col'), may hold values from -0.125 to 0.125
- kernel: float32 [125, 4096], P(None, 'col'), may hold values from -0.625 to 0.625
- cotangent: bfloat16 [2, 16, 4, 16, 2048], P('dp', 'row', None, None, 'col'), may hold values from -2 to 2
Outputs:
- block_output: bfloat16 [2, 16, 4, 16, 2048], P('dp', 'row', None, None, 'col')
- input_grad: bfloat16 [2, 16, 4, 16, 2048], P('dp', 'row', None, None, 'col')
- up_grad: bfloat16 [2048, 4096], P(('dp', 'row'), 'col')
- down_grad: bfloat16 [2048, 4096], P(('dp', 'row'), 'col')
- kernel_grad: float32 [125, 4096], P(None, 'col')
All inputs are finite; a program needn't handle non-finite values.
Results may differ from a plain program's by a relative error of at most 0.012.
Values may be sent and summed in bfloat16 or wider, within the bound.
A program may use at most 128 MiB of HBM per device.

v0:
```python
import jax
import jax.numpy as jnp
from jax import lax
from jax.sharding import PartitionSpec as P


def with_halo(shard, sides, width):
    for axis, dim in sides:
        peers, length = (lax.axis_size(axis), shard.shape[dim])
        up = [(i, (i + 1) % peers) for i in range(peers - 1)]
        down = [(j, i) for i, j in up]
        last = lax.slice_in_dim(shard, length - width, length, axis=dim)
        initial = lax.slice_in_dim(shard, 0, width, axis=dim)
        before = lax.ppermute(last, axis, up)
        after = lax.ppermute(initial, axis, down)
        shard = jnp.concatenate([before, shard, after], axis=dim)
    return shard


def depth_margin(field):
    extended = with_halo(field, (("row", 1),), 2)
    return jnp.pad(extended, ((0, 0), (0, 0), (2, 2), (2, 2), (0, 0)))


def stencil_sum(padded, kernel, mirror):
    planes = padded.shape[1] - 4
    tile_x = padded.shape[2] - 4
    tile_y = padded.shape[3] - 4
    result = jnp.zeros(padded.shape[:1] + (planes, tile_x, tile_y, padded.shape[4]), jnp.float32)
    for depth_step in range(5):
        for row_step in range(5):
            for col_step in range(5):
                first_z = depth_step + mirror * (4 - 2 * depth_step)
                first_x = row_step + mirror * (4 - 2 * row_step)
                first_y = col_step + mirror * (4 - 2 * col_step)
                window = padded[
                    :,
                    first_z : first_z + planes,
                    first_x : first_x + tile_x,
                    first_y : first_y + tile_y,
                    :,
                ]
                result = result + kernel[25 * depth_step + 5 * row_step + col_step] * window
    return result


def kernel_terms(padded, grad_field):
    planes = grad_field.shape[1]
    tile_x = grad_field.shape[2]
    tile_y = grad_field.shape[3]
    grad_wide = grad_field.astype(jnp.float32)
    rows_list = []
    for depth_step in range(5):
        for row_step in range(5):
            for col_step in range(5):
                window = padded[
                    :,
                    depth_step : depth_step + planes,
                    row_step : row_step + tile_x,
                    col_step : col_step + tile_y,
                    :,
                ]
                rows_list.append(jnp.sum(window * grad_wide, axis=(0, 1, 2, 3)))
    return jnp.stack(rows_list)


def column_sum(partial_value, field_shape):
    return lax.psum_scatter(
        partial_value.reshape(field_shape).astype(jnp.bfloat16),
        "col",
        scatter_dimension=4,
        tiled=True,
    ).astype(jnp.float32)


def spread_product(left_rows, right_rows):
    return lax.dot_general(
        left_rows, right_rows, (((0,), (0,)), ((), ())), preferred_element_type=jnp.float32
    )


def on_device(inputs, up_weight, down_weight, kernel, cotangent):
    states, planes, tile_x, tile_y, local_width = inputs.shape
    voxels = states * planes * tile_x * tile_y
    local_hidden = up_weight.shape[1]
    contract_last = (((1,), (1,)), ((), ()))
    input_rows, cotangent_rows = (
        lax.all_gather(inputs, "col", axis=4, tiled=True),
        lax.all_gather(cotangent, "col", axis=4, tiled=True),
    )
    full_width = input_rows.shape[4]
    field_shape = (states, planes, tile_x, tile_y, full_width)
    hidden_shape = (states, planes, tile_x, tile_y, local_hidden)
    flat_inputs = input_rows.reshape(voxels, full_width)
    hidden = jnp.dot(flat_inputs, up_weight, preferred_element_type=jnp.float32).astype(
        jnp.bfloat16
    )
    hidden_pad = depth_margin(hidden.reshape(hidden_shape))
    preact = stencil_sum(hidden_pad, kernel, 0)
    activation = jax.nn.silu(preact).astype(jnp.bfloat16)
    flat_act = activation.reshape(voxels, local_hidden)
    mixed_share = column_sum(
        lax.dot_general(flat_act, down_weight, contract_last, preferred_element_type=jnp.float32),
        field_shape,
    )
    block_output = (inputs.astype(jnp.float32) + mixed_share).astype(jnp.bfloat16)
    flat_cotangent = cotangent_rows.reshape(voxels, full_width)
    act_grad = jnp.dot(flat_cotangent, down_weight, preferred_element_type=jnp.float32).reshape(
        hidden_shape
    )
    logistic = jax.nn.sigmoid(preact)
    preact_grad = (act_grad * logistic * (1.0 + preact * (1.0 - logistic))).astype(jnp.bfloat16)
    grad_pad = depth_margin(preact_grad)
    hidden_grad = stencil_sum(grad_pad, kernel, 1).astype(jnp.bfloat16)
    kernel_grad = lax.psum(
        kernel_terms(hidden_pad, preact_grad).astype(jnp.bfloat16), ("dp", "row")
    ).astype(jnp.float32)
    flat_grad_hidden = hidden_grad.reshape(voxels, local_hidden)
    input_share = column_sum(
        lax.dot_general(
            flat_grad_hidden, up_weight, contract_last, preferred_element_type=jnp.float32
        ),
        field_shape,
    )
    input_grad = (cotangent.astype(jnp.float32) + input_share).astype(jnp.bfloat16)
    both_share = lax.psum_scatter(
        jnp.concatenate(
            [
                spread_product(flat_inputs, flat_grad_hidden),
                spread_product(flat_cotangent, flat_act),
            ],
            axis=1,
        ).astype(jnp.bfloat16),
        ("dp", "row"),
        scatter_dimension=0,
        tiled=True,
    ).astype(jnp.float32)
    up_share = both_share[:, :local_hidden]
    down_share = both_share[:, local_hidden:]
    up_grad = up_share.astype(jnp.bfloat16)
    down_grad = down_share.astype(jnp.bfloat16)
    return (block_output, input_grad, up_grad, down_grad, kernel_grad)


def solution(mesh):
    placed = (
        P("dp", "row", None, None, "col"),
        P(None, "col"),
        P(None, "col"),
        P(None, "col"),
        P("dp", "row", None, None, "col"),
    )
    return jax.shard_map(
        on_device,
        mesh=mesh,
        in_specs=placed,
        out_specs=(
            P("dp", "row", None, None, "col"),
            P("dp", "row", None, None, "col"),
            P(("dp", "row"), "col"),
            P(("dp", "row"), "col"),
            P(None, "col"),
        ),
        check_vma=False,
    )
```

profile of v0, /device:TPU:0, one launch (start us, length us, event | category | flops | bytes accessed | tf_op | source)
XLA Modules:
  0.0 385.0 jit_solution(17823461748566457241)
XLA Ops:
  8.7 1.3 fusion.328
  10.0 2.0 fusion.327
  12.0 1.9 fusion.326
  13.9 1.9 fusion.325
  15.9 2.0 fusion.324
  17.9 22.3 %all-gather.3.cloned.1.call-done = bf16[1,4,4,16,2048]{4,3,2,1,0:T(8,128)(2,1)} async-done(((bf16[1,4,4,16,512]{4,3,2,1,0:T(8,128)(2,1)}), bf16[1,4,4,16,2048]{4,3,2,1,0:T(8,128)(2,1)}) %all-gather.3.cloned.1.call-update) | async-done | bytes 1048592 | tf_op jit(solution)/shard_map/all_gather | solution.py:88
  40.2 3.8 convolution_convert_fusion
  45.8 4.7 %collective-permute-start = (bf16[1,2,4,16,1024]{4,3,2,1,0:T(8,128)(2,1)S(1)}, bf16[1,2,4,16,1024]{4,3,2,1,0:T(8,128)(2,1)S(1)}, u32[]{:S(2)}, u32[]{:S(2)}) collective-permute-start(bf16[1,2,4,16,1024]{4,3,2,1,0:T(8,128)(2,1)S(1)} %get-tuple-element.142), channel_id=1, source_target_pairs={{0,4},{4,8},{8,12},{1,5},{5,9},{9,13},{2,6},{6,10},{10,14},{3,7},{... | collective-permute-start | bytes 786440 | tf_op jit(solution)/shard_map/ppermute | solution.py:14
  51.7 1.4 fusion.329
  53.3 2.3 collective-permute-done.1
  57.1 28.9 %fusion.159 = f32[1,4,4,16,1024]{4,3,2,1,0:T(8,128)} fusion(bf16[1,4,4,16,1024]{4,3,2,1,0:T(8,128)(2,1)S(1)} %bitcast.210, f32[1024]{0:T(1024)S(1)} %bitcast.420, f32[1024]{0:T(1024)S(1)} %bitcast.422, f32[1024]{0:T(1024)} %bitcast.366, f32[1024]{0:T(1024)} %bitcast.368, f32[1024]{0:T(1024)} %bitcast.370, f32[1024]{0:T(1024)} %bitcast.372, ...), kind=kLoop, calls=%fused_computation.406 | loop fusion | flops 99090432 | bytes 65523712 | tf_op jit(solution)/shard_map/add | solution.py:43
  86.1 6.9 %fusion.303 = (bf16[1024]{0:T(1024)(128)(2,1)}, bf16[1024]{0:T(1024)(128)(2,1)}, bf16[1024]{0:T(1024)(128)(2,1)}, bf16[1024]{0:T(1024)(128)(2,1)}, bf16[1024]{0:...) fusion(bf16[1,8,8,20,1024]{4,3,2,1,0:T(8,128)(2,1)S(1)} %select, ...), kind=kOutput, calls=%fused_computation.550 | convolution fusion | flops 1086573568 | bytes 13658112 | tf_op jit(solution)/shard_map/dot_general | solution.py:108
  93.1 3.4 fusion.308
  96.5 3.4 fusion.309
  99.9 3.4 fusion.306
  103.3 3.4 fusion.304
  106.7 3.3 fusion.305
  110.0 3.4 fusion.307
  113.8 2.3 fusion.21
  175.0 10.6 %stack.629 = bf16[125,1024]{1,0:T(8,128)(2,1)} concatenate(bf16[1,1024]{1,0:T(2,128)(2,1)S(1)} %stack.504, bf16[1,1024]{1,0:T(2,128)(2,1)S(1)} %stack.505, bf16[1,1024]{1,0:T(2,128)(2,1)S(1)} %stack.506, bf16[1,1024]{1,0:T(2,128)(2,1)S(1)} %stack.507, bf16[1,1024]{1,0:T(2,128)(2,1)S(1)} %stack.508, bf16[1,1024]{1,0:T(2,128)(2,1)S(1)} %stack.509, bf16[1,1024]{1,0:T(2,128)(2,1)S(1)} %stack.510, ...), dimensions={0} | concatenate | bytes 512000 | tf_op jit(solution)/shard_map/stack | solution.py:64
  187.0 6.4 %collective-permute-start.2 = (bf16[1,2,4,16,1024]{4,3,2,1,0:T(8,128)(2,1)S(1)}, bf16[1,2,4,16,1024]{4,3,2,1,0:T(8,128)(2,1)S(1)}, u32[]{:S(2)}, u32[]{:S(2)}) collective-permute-start(bf16[1,2,4,16,1024]{4,3,2,1,0:T(8,128)(2,1)S(1)} %get-tuple-element.140), channel_id=1, source_target_pairs={{0,4},{4,8},{8,12},{1,5},{5,9},{9,13},{2,6},{6,10},{10,14},{3,7},{... | collective-permute-start | bytes 786440 | tf_op jit(solution)/shard_map/ppermute | solution.py:14
  193.5 4.5 %fusion.10 = bf16[2048,1024]{0,1:T(8,128)(2,1)} fusion(bf16[1,4,4,16,2048]{4,3,2,1,0:T(8,128)(2,1)} %all-gather.5.cloned.1.call-done, f32[1,4,4,16,1024]{4,3,2,1,0:T(8,128)S(1)} %copy-done.7), kind=kOutput, calls=%fused_computation.143 | convolution fusion | flops 1077149696 | bytes 6291456 | tf_op jit(solution)/shard_map/dot_general | solution.py:77
  200.0 30.2 %add_convert_fusion = bf16[1,4,4,16,1024]{4,3,2,1,0:T(8,128)(2,1)S(1)} fusion(bf16[1,4,4,16,1024]{4,3,2,1,0:T(8,128)(2,1)S(1)} %copy-done.1, bf16[1,2,4,16,1024]{4,3,2,1,0:T(8,128)(2,1)S(1)} %collective-permute-done.2, bf16[1,2,4,16,1024]{4,3,2,1,0:T(8,128)(2,1)S(1)} %collective-permute-done.3, bf16[1,8,8,20,1024]{4,3,2,1,0:T(8,128)(2,1)S(1)} %select_maximum_fusion, ...), kind=kLoop, calls=%fused_computation.560 | loop fusion | flops 99352576 | bytes 64999424 | tf_op jit(solution)/shard_map/convert_element_type | solution.py:114
  230.2 4.5 %fusion.18 = bf16[1,4,4,16,2048]{4,3,2,1,0:T(8,128)(2,1)} fusion(bf16[2048,1024]{1,0:T(8,128)(2,1)} %param.6, bf16[1,4,4,16,1024]{4,3,2,1,0:T(8,128)(2,1)S(1)} %add_convert_fusion), kind=kOutput, calls=%fused_computation.151 | convolution fusion | flops 1074266112 | bytes 5767168 | tf_op jit(solution)/shard_map/dot_general | solution.py:120
  234.8 4.5 %fusion.9 = bf16[2048,1024]{0,1:T(8,128)(2,1)} fusion(bf16[1,4,4,16,2048]{4,3,2,1,0:T(8,128)(2,1)} %all-gather.3.cloned.1.call-done, bf16[1,4,4,16,1024]{4,3,2,1,0:T(8,128)(2,1)S(1)} %add_convert_fusion), kind=kOutput, calls=%fused_computation.142 | convolution fusion | flops 1075838976 | bytes 5767168 | tf_op jit(solution)/shard_map/dot_general | solution.py:77
  239.3 8.4 %pad_maximum_fusion = bf16[2048,2048]{0,1:T(8,128)(2,1)} fusion(bf16[2048,1024]{0,1:T(8,128)(2,1)} %fusion.10, bf16[2048,1024]{0,1:T(8,128)(2,1)} %fusion.9), kind=kLoop, calls=%fused_computation.130 | loop fusion | flops 16777216 | bytes 16777216 | tf_op jit(solution)/shard_map/concatenate | solution.py:127
  247.7 1.8 convert_element_type.1202
  249.6 23.6 %reduce-scatter.4.cloned.1.call-done = bf16[1,4,4,16,512]{4,3,2,1,0:T(8,128)(2,1)} async-done(((bf16[1,4,4,16,2048]{4,3,2,1,0:T(8,128)(2,1)}), bf16[1,4,4,16,512]{4,3,2,1,0:T(8,128)(2,1)}) %reduce-scatter.4.cloned.1.call-update) | async-done | bytes 262160 | tf_op jit(solution)/shard_map/reduce_scatter | solution.py:68
  273.2 1.7 add_convert_fusion.2
  274.9 26.2 %reduce-scatter.6.cloned.1.call-done = bf16[1,4,4,16,512]{4,3,2,1,0:T(8,128)(2,1)} async-done(((bf16[1,4,4,16,2048]{4,3,2,1,0:T(8,128)(2,1)}), bf16[1,4,4,16,512]{4,3,2,1,0:T(8,128)(2,1)}) %reduce-scatter.6.cloned.1.call-update) | async-done | bytes 262160 | tf_op jit(solution)/shard_map/reduce_scatter | solution.py:68
  301.1 1.7 add_convert_fusion.1
  302.9 71.9 %reduce-scatter.8.cloned.1.call-done = bf16[256,2048]{0,1:T(8,128)(2,1)} async-done(((bf16[2048,2048]{0,1:T(8,128)(2,1)}), bf16[256,2048]{0,1:T(8,128)(2,1)}) %reduce-scatter.8.cloned.1.call-update) | async-done | bytes 1048592 | tf_op jit(solution)/shard_map/reduce_scatter | solution.py:126
  (465 shorter events, 69.6 us)
Async XLA Ops:
  7.2 33.1 %all-gather.3.cloned.1.call-start = ((), (), s32[]{:S(2)}) async-start(), calls=%async_computation.3 | async-start | bytes 1310720 | tf_op jit(solution)/shard_map/all_gather | solution.py:88
  7.9 78.2 %all-gather.5.cloned.1.call-start = ((), (), s32[]{:S(2)}) async-start(), calls=%async_computation.5 | async-start | bytes 1310720 | tf_op jit(solution)/shard_map/all_gather | solution.py:89
  8.6 239.1 %all-reduce.4.cloned.1.call-start = ((), (), s32[]{:S(2)}) async-start(), calls=%async_computation.8 | async-start | bytes 524288 | tf_op jit(solution)/shard_map/psum | solution.py:115
  44.5 11.1 %collective-permute-start.1 = (bf16[1,2,4,16,1024]{4,3,2,1,0:T(8,128)(2,1)S(1)}, bf16[1,2,4,16,1024]{4,3,2,1,0:T(8,128)(2,1)S(1)}, u32[]{:S(2)}, u32[]{:S(2)}) collective-permute-start(bf16[1,2,4,16,1024]{4,3,2,1,0:T(8,128)(2,1)S(1)} %get-tuple-element.141), channel_id=1, source_target_pairs={{4,0},{8,4},{12,8},{5,1},{9,5},{13,9},{6,2},{10,6},{14,10},{7,3},{... | collective-permute-start | bytes 786440 | tf_op jit(solution)/shard_map/ppermute | solution.py:15
  45.8 9.8 %collective-permute-start = (bf16[1,2,4,16,1024]{4,3,2,1,0:T(8,128)(2,1)S(1)}, bf16[1,2,4,16,1024]{4,3,2,1,0:T(8,128)(2,1)S(1)}, u32[]{:S(2)}, u32[]{:S(2)}) collective-permute-start(bf16[1,2,4,16,1024]{4,3,2,1,0:T(8,128)(2,1)S(1)} %get-tuple-element.142), channel_id=1, source_target_pairs={{0,4},{4,8},{8,12},{1,5},{5,9},{9,13},{2,6},{6,10},{10,14},{3,7},{... | collective-permute-start | bytes 786440 | tf_op jit(solution)/shard_map/ppermute | solution.py:14
  113.5 60.9 %copy-start.140 = (bf16[1024]{0:T(1024)(128)(2,1)S(1)}, bf16[1024]{0:T(1024)(128)(2,1)}, u32[]{:S(2)}) copy-start(bf16[1024]{0:T(1024)(128)(2,1)} %get-tuple-element.96) | copy-start | bytes 6148
  113.6 61.0 %copy-start.139 = (bf16[1024]{0:T(1024)(128)(2,1)S(1)}, bf16[1024]{0:T(1024)(128)(2,1)}, u32[]{:S(2)}) copy-start(bf16[1024]{0:T(1024)(128)(2,1)} %get-tuple-element.97) | copy-start | bytes 6148
  113.6 61.0 %copy-start.138 = (bf16[1024]{0:T(1024)(128)(2,1)S(1)}, bf16[1024]{0:T(1024)(128)(2,1)}, u32[]{:S(2)}) copy-start(bf16[1024]{0:T(1024)(128)(2,1)} %get-tuple-element.98) | copy-start | bytes 6148
  113.6 61.0 %copy-start.136 = (bf16[1024]{0:T(1024)(128)(2,1)S(1)}, bf16[1024]{0:T(1024)(128)(2,1)}, u32[]{:S(2)}) copy-start(bf16[1024]{0:T(1024)(128)(2,1)} %get-tuple-element.99) | copy-start | bytes 6148
  113.6 61.0 %copy-start.137 = (bf16[1024]{0:T(1024)(128)(2,1)S(1)}, bf16[1024]{0:T(1024)(128)(2,1)}, u32[]{:S(2)}) copy-start(bf16[1024]{0:T(1024)(128)(2,1)} %get-tuple-element.47) | copy-start | bytes 6148
  113.6 61.0 %copy-start.135 = (bf16[1024]{0:T(1024)(128)(2,1)S(1)}, bf16[1024]{0:T(1024)(128)(2,1)}, u32[]{:S(2)}) copy-start(bf16[1024]{0:T(1024)(128)(2,1)} %get-tuple-element.48) | copy-start | bytes 6148
  113.6 61.0 %copy-start.134 = (bf16[1024]{0:T(1024)(128)(2,1)S(1)}, bf16[1024]{0:T(1024)(128)(2,1)}, u32[]{:S(2)}) copy-start(bf16[1024]{0:T(1024)(128)(2,1)} %get-tuple-element.49) | copy-start | bytes 6148
  113.6 61.0 %copy-start.133 = (bf16[1024]{0:T(1024)(128)(2,1)S(1)}, bf16[1024]{0:T(1024)(128)(2,1)}, u32[]{:S(2)}) copy-start(bf16[1024]{0:T(1024)(128)(2,1)} %get-tuple-element.50) | copy-start | bytes 6148
  113.6 61.0 %copy-start.132 = (bf16[1024]{0:T(1024)(128)(2,1)S(1)}, bf16[1024]{0:T(1024)(128)(2,1)}, u32[]{:S(2)}) copy-start(bf16[1024]{0:T(1024)(128)(2,1)} %get-tuple-element.51) | copy-start | bytes 6148
  113.6 61.1 %copy-start.131 = (bf16[1024]{0:T(1024)(128)(2,1)S(1)}, bf16[1024]{0:T(1024)(128)(2,1)}, u32[]{:S(2)}) copy-start(bf16[1024]{0:T(1024)(128)(2,1)} %get-tuple-element.52) | copy-start | bytes 6148
  113.7 61.1 %copy-start.130 = (bf16[1024]{0:T(1024)(128)(2,1)S(1)}, bf16[1024]{0:T(1024)(128)(2,1)}, u32[]{:S(2)}) copy-start(bf16[1024]{0:T(1024)(128)(2,1)} %get-tuple-element.53) | copy-start | bytes 6148
  113.7 61.1 %copy-start.129 = (bf16[1024]{0:T(1024)(128)(2,1)S(1)}, bf16[1024]{0:T(1024)(128)(2,1)}, u32[]{:S(2)}) copy-start(bf16[1024]{0:T(1024)(128)(2,1)} %get-tuple-element.54) | copy-start | bytes 6148
  113.7 61.1 %copy-start.128 = (bf16[1024]{0:T(1024)(128)(2,1)S(1)}, bf16[1024]{0:T(1024)(128)(2,1)}, u32[]{:S(2)}) copy-start(bf16[1024]{0:T(1024)(128)(2,1)} %get-tuple-element.55) | copy-start | bytes 6148
  113.7 61.1 %copy-start.127 = (bf16[1024]{0:T(1024)(128)(2,1)S(1)}, bf16[1024]{0:T(1024)(128)(2,1)}, u32[]{:S(2)}) copy-start(bf16[1024]{0:T(1024)(128)(2,1)} %get-tuple-element.56) | copy-start | bytes 6148
  113.7 61.1 %copy-start.126 = (bf16[1024]{0:T(1024)(128)(2,1)S(1)}, bf16[1024]{0:T(1024)(128)(2,1)}, u32[]{:S(2)}) copy-start(bf16[1024]{0:T(1024)(128)(2,1)} %get-tuple-element.57) | copy-start | bytes 6148
  113.7 61.1 %copy-start.125 = (bf16[1024]{0:T(1024)(128)(2,1)S(1)}, bf16[1024]{0:T(1024)(128)(2,1)}, u32[]{:S(2)}) copy-start(bf16[1024]{0:T(1024)(128)(2,1)} %get-tuple-element.58) | copy-start | bytes 6148
  113.7 61.2 %copy-start.124 = (bf16[1024]{0:T(1024)(128)(2,1)S(1)}, bf16[1024]{0:T(1024)(128)(2,1)}, u32[]{:S(2)}) copy-start(bf16[1024]{0:T(1024)(128)(2,1)} %get-tuple-element.59) | copy-start | bytes 6148
  113.7 61.2 %copy-start.123 = (bf16[1024]{0:T(1024)(128)(2,1)S(1)}, bf16[1024]{0:T(1024)(128)(2,1)}, u32[]{:S(2)}) copy-start(bf16[1024]{0:T(1024)(128)(2,1)} %get-tuple-element.60) | copy-start | bytes 6148
  113.7 61.2 %copy-start.122 = (bf16[1024]{0:T(1024)(128)(2,1)S(1)}, bf16[1024]{0:T(1024)(128)(2,1)}, u32[]{:S(2)}) copy-start(bf16[1024]{0:T(1024)(128)(2,1)} %get-tuple-element.61) | copy-start | bytes 6148
  113.7 61.2 %copy-start.121 = (bf16[1024]{0:T(1024)(128)(2,1)S(1)}, bf16[1024]{0:T(1024)(128)(2,1)}, u32[]{:S(2)}) copy-start(bf16[1024]{0:T(1024)(128)(2,1)} %get-tuple-element.62) | copy-start | bytes 6148
  113.8 61.2 %copy-start.120 = (bf16[1024]{0:T(1024)(128)(2,1)S(1)}, bf16[1024]{0:T(1024)(128)(2,1)}, u32[]{:S(2)}) copy-start(bf16[1024]{0:T(1024)(128)(2,1)} %get-tuple-element.63) | copy-start | bytes 6148
  116.0 77.5 %copy-start.7 = (f32[1,4,4,16,1024]{4,3,2,1,0:T(8,128)S(1)}, f32[1,4,4,16,1024]{4,3,2,1,0:T(8,128)}, u32[]{:S(2)}) copy-start(f32[1,4,4,16,1024]{4,3,2,1,0:T(8,128)} %fusion.159) | copy-start | bytes 3145732
  185.6 87.5 %reduce-scatter.4.cloned.1.call-start = ((), (), s32[]{:S(2)}) async-start(), calls=%async_computation.4 | async-start | bytes 1310720 | tf_op jit(solution)/shard_map/reduce_scatter | solution.py:68
  185.7 12.7 %collective-permute-start.3 = (bf16[1,2,4,16,1024]{4,3,2,1,0:T(8,128)(2,1)S(1)}, bf16[1,2,4,16,1024]{4,3,2,1,0:T(8,128)(2,1)S(1)}, u32[]{:S(2)}, u32[]{:S(2)}) collective-permute-start(bf16[1,2,4,16,1024]{4,3,2,1,0:T(8,128)(2,1)S(1)} %get-tuple-element.139), channel_id=1, source_target_pairs={{4,0},{8,4},{12,8},{5,1},{9,5},{13,9},{6,2},{10,6},{14,10},{7,3},{... | collective-permute-start | bytes 786440 | tf_op jit(solution)/shard_map/ppermute | solution.py:15
  187.0 11.4 %collective-permute-start.2 = (bf16[1,2,4,16,1024]{4,3,2,1,0:T(8,128)(2,1)S(1)}, bf16[1,2,4,16,1024]{4,3,2,1,0:T(8,128)(2,1)S(1)}, u32[]{:S(2)}, u32[]{:S(2)}) collective-permute-start(bf16[1,2,4,16,1024]{4,3,2,1,0:T(8,128)(2,1)S(1)} %get-tuple-element.140), channel_id=1, source_target_pairs={{0,4},{4,8},{8,12},{1,5},{5,9},{9,13},{2,6},{6,10},{10,14},{3,7},{... | collective-permute-start | bytes 786440 | tf_op jit(solution)/shard_map/ppermute | solution.py:14
  193.5 107.7 %reduce-scatter.6.cloned.1.call-start = ((), (), s32[]{:S(2)}) async-start(), calls=%async_computation.6 | async-start | bytes 1310720 | tf_op jit(solution)/shard_map/reduce_scatter | solution.py:68
  234.8 140.0 %reduce-scatter.8.cloned.1.call-start = ((), (), s32[]{:S(2)}) async-start(), calls=%async_computation.7 | async-start | bytes 9437184 | tf_op jit(solution)/shard_map/reduce_scatter | solution.py:126
  (134 other events, 1667.5 us)
Sparse Core Ops, SparseCore 0:
  9.6 30.6 all-gather.2
  41.8 27.4 all-gather.4
  185.8 58.5 all-reduce.3
  246.6 26.5 reduce-scatter.3
  275.3 25.7 reduce-scatter.5
  304.9 69.9 reduce-scatter.7
where the time goes:
time: 388 us; the launch traced here: 385 us
  waiting for transfers between devices  148 us (38%)
  other arithmetic  95.6 us (25%)
  local copies, waits for them, and re-layouts  84.1 us (22%)
  matrix products  26.5 us (7%)
  between operations  16.9 us (4%)
  starting transfers between devices  14 us (4%)
    reduce_scatter x1, waiting for transfers between devices, on_device(): lax.psum_scatter(jnp.concatenate([spread_product(flat_inputs, flat_grad_h...  71.9 us
    another operation x126, local copies, waits for them, and re-layouts, kernel_terms(): return jnp.stack(rows_list)  68.4 us
    reduce_scatter x2, waiting for transfers between devices, column_sum(): lax.psum_scatter(partial_value.reshape(field_shape).astype(jnp.bfloat16),...  49.8 us
    convert_element_type x1, other arithmetic, on_device(): hidden_grad = stencil_sum(grad_pad, kernel, 1).astype(jnp.bfloat16)  30.2 us
    add x1, other arithmetic, stencil_sum(): result = result + kernel[25 * depth_step + 5 * row_step + col_step] * window  28.9 us
    all_gather x1, waiting for transfers between devices, on_device(): lax.all_gather(inputs, 'col', axis=4, tiled=True)  22.3 us
    reduce_sum x7, other arithmetic, kernel_terms(): rows_list.append(jnp.sum(window * grad_wide, axis=(0, 1, 2, 3)))  20.7 us
    slice x7, local copies, waits for them, and re-layouts, stencil_sum(): result = result + kernel[25 * depth_step + 5 * row_step + col_step] * window  11.7 us
  transfers between devices with their start and end apart: 10, of which 5 were waited for; matrix products, arithmetic and copies ran while one was open for 27% of the time, Pallas kernels for 0%

commit v1 on v0

--- a/solution.py
+++ b/solution.py
@@ -80,12 +80,27 @@
 
 
 def on_device(inputs, up_weight, down_weight, kernel, cotangent):
+
+    def deliver_case(message, out_dim):
+        reached, reply = (jax.lax.axis_size("col"), jax.lax.axis_index("col"))
+        carry_out, state_next = (message, 1)
+        while state_next < reached:
+            vals = []
+            for j0 in range(reached):
+                vals.append((j0, j0 ^ state_next))
+            next_value = jax.lax.ppermute(carry_out, "col", vals)
+            right_arr = jnp.concatenate([carry_out, next_value], out_dim)
+            known = jnp.concatenate([next_value, carry_out], out_dim)
+            carry_out = jnp.where(reply & state_next == 0, right_arr, known)
+            state_next = 2 * state_next
+        return carry_out
+
     states, planes, tile_x, tile_y, local_width = inputs.shape
     voxels = states * planes * tile_x * tile_y
     local_hidden = up_weight.shape[1]
     contract_last = (((1,), (1,)), ((), ()))
     input_rows, cotangent_rows = (
-        lax.all_gather(inputs, "col", axis=4, tiled=True),
+        deliver_case(inputs, 4),
         lax.all_gather(cotangent, "col", axis=4, tiled=True),
     )
     full_width = input_rows.shape[4]

time: 388 us -> 345 us (0.89)
  local copies, waits for them, and re-layouts: 84.1 us -> 27.4 us
  waiting for transfers between devices: 148 us -> 157 us
  starting transfers between devices: 14 us -> 19.9 us
    another operation x126, local copies, waits for them, and re-layouts: 68.4 us -> 11.3 us  [kernel_terms(): return jnp.stack(rows_list)]
    ppermute x0 -> x2, waiting for transfers between devices: none -> 34.4 us  [deliver_case(): next_value = jax.lax.ppermute(carry_out, 'col', vals)]
    all_gather x1 -> x0, waiting for transfers between devices: 22.3 us -> none  [on_device(): lax.all_gather(inputs, 'col', axis=4, tiled=True)]
    ppermute x0 -> x2, starting transfers between devices: none -> 5.74 us  [deliver_case(): next_value = jax.lax.ppermute(carry_out, 'col', vals)]
  transfers between devices with their start and end apart: 10 -> 11, of which waited for: 5 -> 5; matrix products, arithmetic and copies ran while one was open for 27% -> 33% of each run, Pallas kernels for 0% -> 0%
where the time goes in v1:
time: 345 us; the launch traced here: 344 us
  waiting for transfers between devices  157 us (46%)
  other arithmetic  96.2 us (28%)
  local copies, waits for them, and re-layouts  27.4 us (8%)
  matrix products  26.9 us (8%)
  starting transfers between devices  19.9 us (6%)
  between operations  16.6 us (5%)
    reduce_scatter x1, waiting for transfers between devices, on_device(): lax.psum_scatter(jnp.concatenate([spread_product(flat_inputs, flat_grad_h...  71.9 us
    reduce_scatter x2, waiting for transfers between devices, column_sum(): lax.psum_scatter(partial_value.reshape(field_shape).astype(jnp.bfloat16),...  47.3 us
    ppermute x2, waiting for transfers between devices, deliver_case(): next_value = jax.lax.ppermute(carry_out, 'col', vals)  34.4 us
    convert_element_type x1, other arithmetic, on_device(): hidden_grad = stencil_sum(grad_pad, kernel, 1).astype(jnp.bfloat16)  30.2 us
    add x1, other arithmetic, stencil_sum(): result = result + kernel[25 * depth_step + 5 * row_step + col_step] * window  29.6 us
    reduce_sum x7, other arithmetic, kernel_terms(): rows_list.append(jnp.sum(window * grad_wide, axis=(0, 1, 2, 3)))  17.2 us
    slice x7, local copies, waits for them, and re-layouts, stencil_sum(): result = result + kernel[25 * depth_step + 5 * row_step + col_step] * window  12.3 us
    another operation x126, local copies, waits for them, and re-layouts, kernel_terms(): return jnp.stack(rows_list)  11.3 us
  transfers between devices with their start and end apart: 11, of which 5 were waited for; matrix products, arithmetic and copies ran while one was open for 33% of the time, Pallas kernels for 0%

profile of v1, /device:TPU:0, one launch (start us, length us, event | category | flops | bytes accessed | tf_op | source)
XLA Modules:
  0.0 343.7 jit_solution(17093727181631470255)
XLA Ops:
  7.9 3.1 collective-permute-start
  12.3 2.0 fusion.339
  14.3 1.9 fusion.338
  19.1 2.7 collective-permute-start.1
  21.7 2.0 fusion.336
  23.9 2.0 fusion.341
  27.2 34.4 %collective-permute-done.1 = bf16[1,4,4,16,1024]{4,3,2,1,0:T(8,128)(2,1)S(1)} collective-permute-done((bf16[1,4,4,16,1024]{4,3,2,1,0:T(8,128)(2,1)S(1)}, bf16[1,4,4,16,1024]{4,3,2,1,0:T(8,128)(2,1)S(1)}, u32[]{:S(2)}, u32[]{:S(2)}) %collective-permute-start.1) | collective-permute-done | bytes 524320 | tf_op jit(solution)/shard_map/ppermute | solution.py:91
  61.5 3.7 %convolution_convert_fusion = bf16[256,1024]{1,0:T(8,128)(2,1)S(1)} fusion(bf16[2048,1024]{1,0:T(8,128)(2,1)} %param.6, bf16[256,1024]{1,0:T(8,128)(2,1)S(1)} %bitcast.399, bf16[256,1024]{1,0:T(8,128)(2,1)S(1)} %maximum_select_fusion.4, pred[]{:T(512)S(6)} %eq.6), kind=kOutput, calls=%fused_computation.281 | convolution fusion | flops 1078722560 | bytes 5767169 | tf_op jit(solution)/shard_map/dot_general | solution.py:110
  66.9 4.7 %collective-permute-start.2 = (bf16[1,2,4,16,1024]{4,3,2,1,0:T(8,128)(2,1)S(1)}, bf16[1,2,4,16,1024]{4,3,2,1,0:T(8,128)(2,1)S(1)}, u32[]{:S(2)}, u32[]{:S(2)}) collective-permute-start(bf16[1,2,4,16,1024]{4,3,2,1,0:T(8,128)(2,1)S(1)} %get-tuple-element.142), channel_id=1, source_target_pairs={{0,4},{4,8},{8,12},{1,5},{5,9},{9,13},{2,6},{6,10},{10,14},{3,7},{... | collective-permute-start | bytes 786440 | tf_op jit(solution)/shard_map/ppermute | solution.py:14
  74.4 2.4 collective-permute-done.3
  78.2 29.6 %fusion.158 = f32[1,4,4,16,1024]{4,3,2,1,0:T(8,128)} fusion(bf16[1,4,4,16,1024]{4,3,2,1,0:T(8,128)(2,1)S(1)} %bitcast.207, f32[1024]{0:T(1024)} %bitcast.128, f32[1024]{0:T(1024)} %bitcast.127, f32[1024]{0:T(1024)S(1)} %bitcast.367, f32[1024]{0:T(1024)S(1)} %bitcast.369, f32[1024]{0:T(1024)S(1)} %bitcast.371, f32[1024]{0:T(1024)S(1)} %bitcast.373, ...), kind=kLoop, calls=%fused_computation.405 | loop fusion | flops 99090432 | bytes 65523712 | tf_op jit(solution)/shard_map/add | solution.py:43
  107.8 6.3 %fusion.302 = (bf16[1024]{0:T(1024)(128)(2,1)S(1)}, bf16[1024]{0:T(1024)(128)(2,1)S(1)}, bf16[1024]{0:T(1024)(128)(2,1)S(1)}, bf16[1024]{0:T(1024)(128)(2,1)S(1)...) fusion(bf16[1,8,8,20,1024]{4,3,2,1,0:T(8,128)(2,1)S(1)} %select, ...), kind=kOutput, calls=%fused_computation.549 | convolution fusion | flops 1086573568 | bytes 13658112 | tf_op jit(solution)/shard_map/dot_general | solution.py:123
  114.2 2.8 fusion.307
  117.0 2.8 fusion.308
  119.8 3.0 fusion.305
  122.8 2.8 fusion.303
  125.6 2.6 fusion.304
  128.3 2.8 fusion.306
  133.2 10.6 %stack.629 = bf16[125,1024]{1,0:T(8,128)(2,1)} concatenate(bf16[1,1024]{1,0:T(2,128)(2,1)S(1)} %stack.504, bf16[1,1024]{1,0:T(2,128)(2,1)S(1)} %stack.505, bf16[1,1024]{1,0:T(2,128)(2,1)S(1)} %stack.506, bf16[1,1024]{1,0:T(2,128)(2,1)S(1)} %stack.507, bf16[1,1024]{1,0:T(2,128)(2,1)S(1)} %stack.508, bf16[1,1024]{1,0:T(2,128)(2,1)S(1)} %stack.509, bf16[1,1024]{1,0:T(2,128)(2,1)S(1)} %stack.510, ...), dimensions={0} | concatenate | bytes 512000 | tf_op jit(solution)/shard_map/stack | solution.py:64
  145.2 6.5 %collective-permute-start.4 = (bf16[1,2,4,16,1024]{4,3,2,1,0:T(8,128)(2,1)S(1)}, bf16[1,2,4,16,1024]{4,3,2,1,0:T(8,128)(2,1)S(1)}, u32[]{:S(2)}, u32[]{:S(2)}) collective-permute-start(bf16[1,2,4,16,1024]{4,3,2,1,0:T(8,128)(2,1)S(1)} %get-tuple-element.140), channel_id=1, source_target_pairs={{0,4},{4,8},{8,12},{1,5},{5,9},{9,13},{2,6},{6,10},{10,14},{3,7},{... | collective-permute-start | bytes 786440 | tf_op jit(solution)/shard_map/ppermute | solution.py:14
  151.7 4.5 %fusion.20 = bf16[1,4,4,16,2048]{4,3,2,1,0:T(8,128)(2,1)} fusion(bf16[2048,1024]{1,0:T(8,128)(2,1)} %param.7, f32[1,4,4,16,1024]{4,3,2,1,0:T(8,128)S(1)} %copy-done.9), kind=kOutput, calls=%fused_computation.151 | convolution fusion | flops 1075576832 | bytes 6291456 | tf_op jit(solution)/shard_map/dot_general | solution.py:118
  158.1 30.2 %add_convert_fusion = bf16[1,4,4,16,1024]{4,3,2,1,0:T(8,128)(2,1)S(1)} fusion(bf16[1,4,4,16,1024]{4,3,2,1,0:T(8,128)(2,1)S(1)} %copy-done.1, bf16[1,2,4,16,1024]{4,3,2,1,0:T(8,128)(2,1)S(1)} %collective-permute-done.4, bf16[1,2,4,16,1024]{4,3,2,1,0:T(8,128)(2,1)S(1)} %collective-permute-done.5, bf16[1,8,8,20,1024]{4,3,2,1,0:T(8,128)(2,1)S(1)} %select_maximum_fusion, ...), kind=kLoop, calls=%fused_computation.570 | loop fusion | flops 99352576 | bytes 64999424 | tf_op jit(solution)/shard_map/convert_element_type | solution.py:129
  188.4 4.5 %fusion.17 = bf16[1,4,4,16,2048]{4,3,2,1,0:T(8,128)(2,1)} fusion(bf16[2048,1024]{1,0:T(8,128)(2,1)} %param.6, bf16[1,4,4,16,1024]{4,3,2,1,0:T(8,128)(2,1)S(1)} %add_convert_fusion), kind=kOutput, calls=%fused_computation.150 | convolution fusion | flops 1074266112 | bytes 5767168 | tf_op jit(solution)/shard_map/dot_general | solution.py:135
  193.0 4.6 %fusion.9 = bf16[2048,1024]{0,1:T(8,128)(2,1)} fusion(bf16[1,4,4,16,2048]{4,3,2,1,0:T(8,128)(2,1)} %all-gather.2.cloned.1.call-done, f32[1,4,4,16,1024]{4,3,2,1,0:T(8,128)S(1)} %copy-done.9), kind=kOutput, calls=%fused_computation.142 | convolution fusion | flops 1077149696 | bytes 6291456 | tf_op jit(solution)/shard_map/dot_general | solution.py:77
  197.6 3.3 bitcast_convert_fusion.1
  200.9 8.4 %pad_maximum_fusion = bf16[2048,2048]{0,1:T(8,128)(2,1)} fusion(bf16[2048,1024]{0,1:T(8,128)(2,1)} %fusion.9, bf16[2048,1024]{0,1:T(8,128)(2,1)} %bitcast_convert_fusion.1), kind=kLoop, calls=%fused_computation.130 | loop fusion | flops 16777216 | bytes 16777216 | tf_op jit(solution)/shard_map/concatenate | solution.py:142
  209.3 1.8 convert_element_type.1202
  211.1 21.1 %reduce-scatter.4.cloned.1.call-done = bf16[1,4,4,16,512]{4,3,2,1,0:T(8,128)(2,1)} async-done(((bf16[1,4,4,16,2048]{4,3,2,1,0:T(8,128)(2,1)}), bf16[1,4,4,16,512]{4,3,2,1,0:T(8,128)(2,1)}) %reduce-scatter.4.cloned.1.call-update) | async-done | bytes 262160 | tf_op jit(solution)/shard_map/reduce_scatter | solution.py:68
  232.2 1.7 add_convert_fusion.2
  234.0 26.2 %reduce-scatter.6.cloned.1.call-done = bf16[1,4,4,16,512]{4,3,2,1,0:T(8,128)(2,1)} async-done(((bf16[1,4,4,16,2048]{4,3,2,1,0:T(8,128)(2,1)}), bf16[1,4,4,16,512]{4,3,2,1,0:T(8,128)(2,1)}) %reduce-scatter.6.cloned.1.call-update) | async-done | bytes 262160 | tf_op jit(solution)/shard_map/reduce_scatter | solution.py:68
  260.2 1.7 add_convert_fusion.1
  261.9 71.9 %reduce-scatter.8.cloned.1.call-done = bf16[256,2048]{0,1:T(8,128)(2,1)} async-done(((bf16[2048,2048]{0,1:T(8,128)(2,1)}), bf16[256,2048]{0,1:T(8,128)(2,1)}) %reduce-scatter.8.cloned.1.call-update) | async-done | bytes 1048592 | tf_op jit(solution)/shard_map/reduce_scatter | solution.py:141
  (377 shorter events, 18.4 us)
Async XLA Ops:
  7.2 100.7 %all-gather.2.cloned.1.call-start = ((), (), s32[]{:S(2)}) async-start(), calls=%async_computation.4 | async-start | bytes 1310720 | tf_op jit(solution)/shard_map/all_gather | solution.py:104
  7.9 201.4 %all-reduce.4.cloned.1.call-start = ((), (), s32[]{:S(2)}) async-start(), calls=%async_computation.7 | async-start | bytes 524288 | tf_op jit(solution)/shard_map/psum | solution.py:130
  7.9 9.9 %collective-permute-start = (bf16[1,4,4,16,512]{4,3,2,1,0:T(8,128)(2,1)}, bf16[1,4,4,16,512]{4,3,2,1,0:T(8,128)(2,1)S(1)}, u32[]{:S(2)}, u32[]{:S(2)}) collective-permute-start(bf16[1,4,4,16,512]{4,3,2,1,0:T(8,128)(2,1)} %param.5), channel_id=1, source_target_pairs={{0,1},{1,0},{2,3},{3,2},{4,5},{5,4},{6,7},{7,6},{8,9},{9,8},{10,11... | collective-permute-start | bytes 786440 | tf_op jit(solution)/shard_map/ppermute | solution.py:91
  17.6 60.0 %copy-start.54 = (f32[1,1024]{1,0:T(1,128)}, f32[1,1024]{1,0:T(1,128)S(1)}, u32[]{:S(2)}) copy-start(f32[1,1024]{1,0:T(1,128)S(1)} %get-tuple-element.162) | copy-start | bytes 12292
  17.6 60.0 %copy-start.56 = (f32[1,1024]{1,0:T(1,128)}, f32[1,1024]{1,0:T(1,128)S(1)}, u32[]{:S(2)}) copy-start(f32[1,1024]{1,0:T(1,128)S(1)} %get-tuple-element.163) | copy-start | bytes 12292
  17.6 60.0 %copy-start.58 = (f32[1,1024]{1,0:T(1,128)}, f32[1,1024]{1,0:T(1,128)S(1)}, u32[]{:S(2)}) copy-start(f32[1,1024]{1,0:T(1,128)S(1)} %get-tuple-element.164) | copy-start | bytes 12292
  17.7 60.0 %copy-start.60 = (f32[1,1024]{1,0:T(1,128)}, f32[1,1024]{1,0:T(1,128)S(1)}, u32[]{:S(2)}) copy-start(f32[1,1024]{1,0:T(1,128)S(1)} %get-tuple-element.165) | copy-start | bytes 12292
  17.7 60.0 %copy-start.62 = (f32[1,1024]{1,0:T(1,128)}, f32[1,1024]{1,0:T(1,128)S(1)}, u32[]{:S(2)}) copy-start(f32[1,1024]{1,0:T(1,128)S(1)} %get-tuple-element.166) | copy-start | bytes 12292
  17.7 60.0 %copy-start.64 = (f32[1,1024]{1,0:T(1,128)}, f32[1,1024]{1,0:T(1,128)S(1)}, u32[]{:S(2)}) copy-start(f32[1,1024]{1,0:T(1,128)S(1)} %get-tuple-element.167) | copy-start | bytes 12292
  17.7 60.0 %copy-start.66 = (f32[1,1024]{1,0:T(1,128)}, f32[1,1024]{1,0:T(1,128)S(1)}, u32[]{:S(2)}) copy-start(f32[1,1024]{1,0:T(1,128)S(1)} %get-tuple-element.168) | copy-start | bytes 12292
  17.7 60.0 %copy-start.68 = (f32[1,1024]{1,0:T(1,128)}, f32[1,1024]{1,0:T(1,128)S(1)}, u32[]{:S(2)}) copy-start(f32[1,1024]{1,0:T(1,128)S(1)} %get-tuple-element.169) | copy-start | bytes 12292
  17.7 60.0 %copy-start.70 = (f32[1,1024]{1,0:T(1,128)}, f32[1,1024]{1,0:T(1,128)S(1)}, u32[]{:S(2)}) copy-start(f32[1,1024]{1,0:T(1,128)S(1)} %get-tuple-element.170) | copy-start | bytes 12292
  17.7 60.0 %copy-start.72 = (f32[1,1024]{1,0:T(1,128)}, f32[1,1024]{1,0:T(1,128)S(1)}, u32[]{:S(2)}) copy-start(f32[1,1024]{1,0:T(1,128)S(1)} %get-tuple-element.171) | copy-start | bytes 12292
  17.7 60.0 %copy-start.74 = (f32[1,1024]{1,0:T(1,128)}, f32[1,1024]{1,0:T(1,128)S(1)}, u32[]{:S(2)}) copy-start(f32[1,1024]{1,0:T(1,128)S(1)} %get-tuple-element.172) | copy-start | bytes 12292
  17.7 60.0 %copy-start.76 = (f32[1,1024]{1,0:T(1,128)}, f32[1,1024]{1,0:T(1,128)S(1)}, u32[]{:S(2)}) copy-start(f32[1,1024]{1,0:T(1,128)S(1)} %get-tuple-element.173) | copy-start | bytes 12292
  17.7 60.0 %copy-start.78 = (f32[1,1024]{1,0:T(1,128)}, f32[1,1024]{1,0:T(1,128)S(1)}, u32[]{:S(2)}) copy-start(f32[1,1024]{1,0:T(1,128)S(1)} %get-tuple-element.174) | copy-start | bytes 12292
  17.8 60.0 %copy-start.80 = (f32[1,1024]{1,0:T(1,128)}, f32[1,1024]{1,0:T(1,128)S(1)}, u32[]{:S(2)}) copy-start(f32[1,1024]{1,0:T(1,128)S(1)} %get-tuple-element.175) | copy-start | bytes 12292
  17.8 60.0 %copy-start.82 = (f32[1,1024]{1,0:T(1,128)}, f32[1,1024]{1,0:T(1,128)S(1)}, u32[]{:S(2)}) copy-start(f32[1,1024]{1,0:T(1,128)S(1)} %get-tuple-element.176) | copy-start | bytes 12292
  17.8 60.0 %copy-start.84 = (f32[1,1024]{1,0:T(1,128)}, f32[1,1024]{1,0:T(1,128)S(1)}, u32[]{:S(2)}) copy-start(f32[1,1024]{1,0:T(1,128)S(1)} %get-tuple-element.177) | copy-start | bytes 12292
  17.8 60.0 %copy-start.86 = (f32[1,1024]{1,0:T(1,128)}, f32[1,1024]{1,0:T(1,128)S(1)}, u32[]{:S(2)}) copy-start(f32[1,1024]{1,0:T(1,128)S(1)} %get-tuple-element.178) | copy-start | bytes 12292
  17.8 60.0 %copy-start.88 = (f32[1,1024]{1,0:T(1,128)}, f32[1,1024]{1,0:T(1,128)S(1)}, u32[]{:S(2)}) copy-start(f32[1,1024]{1,0:T(1,128)S(1)} %get-tuple-element.179) | copy-start | bytes 12292
  17.8 60.0 %copy-start.90 = (f32[1,1024]{1,0:T(1,128)}, f32[1,1024]{1,0:T(1,128)S(1)}, u32[]{:S(2)}) copy-start(f32[1,1024]{1,0:T(1,128)S(1)} %get-tuple-element.180) | copy-start | bytes 12292
  19.1 42.4 %collective-permute-start.1 = (bf16[1,4,4,16,1024]{4,3,2,1,0:T(8,128)(2,1)S(1)}, bf16[1,4,4,16,1024]{4,3,2,1,0:T(8,128)(2,1)S(1)}, u32[]{:S(2)}, u32[]{:S(2)}) collective-permute-start(bf16[1,4,4,16,1024]{4,3,2,1,0:T(8,128)(2,1)S(1)} %maximum_select_fusion.5), channel_id=1, source_target_pairs={{0,2},{1,3},{2,0},{3,1},{4,6},{5,7},{6,4},{7,5},{8,10},{9,11},{10,... | collective-permute-start | bytes 1572872 | tf_op jit(solution)/shard_map/ppermute | solution.py:91
  23.7 54.0 %copy-start.92 = (f32[1,1024]{1,0:T(1,128)}, f32[1,1024]{1,0:T(1,128)S(1)}, u32[]{:S(2)}) copy-start(f32[1,1024]{1,0:T(1,128)S(1)} %get-tuple-element.144) | copy-start | bytes 12292
  23.8 54.0 %copy-start.93 = (f32[1,1024]{1,0:T(1,128)}, f32[1,1024]{1,0:T(1,128)S(1)}, u32[]{:S(2)}) copy-start(f32[1,1024]{1,0:T(1,128)S(1)} %get-tuple-element.145) | copy-start | bytes 12292
  65.5 11.2 %collective-permute-start.3 = (bf16[1,2,4,16,1024]{4,3,2,1,0:T(8,128)(2,1)S(1)}, bf16[1,2,4,16,1024]{4,3,2,1,0:T(8,128)(2,1)S(1)}, u32[]{:S(2)}, u32[]{:S(2)}) collective-permute-start(bf16[1,2,4,16,1024]{4,3,2,1,0:T(8,128)(2,1)S(1)} %get-tuple-element.141), channel_id=1, source_target_pairs={{4,0},{8,4},{12,8},{5,1},{9,5},{13,9},{6,2},{10,6},{14,10},{7,3},{... | collective-permute-start | bytes 786440 | tf_op jit(solution)/shard_map/ppermute | solution.py:15
  66.9 9.8 %collective-permute-start.2 = (bf16[1,2,4,16,1024]{4,3,2,1,0:T(8,128)(2,1)S(1)}, bf16[1,2,4,16,1024]{4,3,2,1,0:T(8,128)(2,1)S(1)}, u32[]{:S(2)}, u32[]{:S(2)}) collective-permute-start(bf16[1,2,4,16,1024]{4,3,2,1,0:T(8,128)(2,1)S(1)} %get-tuple-element.142), channel_id=1, source_target_pairs={{0,4},{4,8},{8,12},{1,5},{5,9},{9,13},{2,6},{6,10},{10,14},{3,7},{... | collective-permute-start | bytes 786440 | tf_op jit(solution)/shard_map/ppermute | solution.py:14
  143.8 88.4 %reduce-scatter.4.cloned.1.call-start = ((), (), s32[]{:S(2)}) async-start(), calls=%async_computation.3 | async-start | bytes 1310720 | tf_op jit(solution)/shard_map/reduce_scatter | solution.py:68
  143.9 12.7 %collective-permute-start.5 = (bf16[1,2,4,16,1024]{4,3,2,1,0:T(8,128)(2,1)S(1)}, bf16[1,2,4,16,1024]{4,3,2,1,0:T(8,128)(2,1)S(1)}, u32[]{:S(2)}, u32[]{:S(2)}) collective-permute-start(bf16[1,2,4,16,1024]{4,3,2,1,0:T(8,128)(2,1)S(1)} %get-tuple-element.139), channel_id=1, source_target_pairs={{4,0},{8,4},{12,8},{5,1},{9,5},{13,9},{6,2},{10,6},{14,10},{7,3},{... | collective-permute-start | bytes 786440 | tf_op jit(solution)/shard_map/ppermute | solution.py:15
  145.2 11.4 %collective-permute-start.4 = (bf16[1,2,4,16,1024]{4,3,2,1,0:T(8,128)(2,1)S(1)}, bf16[1,2,4,16,1024]{4,3,2,1,0:T(8,128)(2,1)S(1)}, u32[]{:S(2)}, u32[]{:S(2)}) collective-permute-start(bf16[1,2,4,16,1024]{4,3,2,1,0:T(8,128)(2,1)S(1)} %get-tuple-element.140), channel_id=1, source_target_pairs={{0,4},{4,8},{8,12},{1,5},{5,9},{9,13},{2,6},{6,10},{10,14},{3,7},{... | collective-permute-start | bytes 786440 | tf_op jit(solution)/shard_map/ppermute | solution.py:14
  156.5 103.7 %reduce-scatter.6.cloned.1.call-start = ((), (), s32[]{:S(2)}) async-start(), calls=%async_computation.5 | async-start | bytes 1310720 | tf_op jit(solution)/shard_map/reduce_scatter | solution.py:68
  192.9 140.9 %reduce-scatter.8.cloned.1.call-start = ((), (), s32[]{:S(2)}) async-start(), calls=%async_computation.6 | async-start | bytes 9437184 | tf_op jit(solution)/shard_map/reduce_scatter | solution.py:141
  (89 other events, 1289.6 us)
Sparse Core Ops, SparseCore 0:
  9.6 49.9 all-gather.1
  143.9 59.2 all-reduce.3
  205.6 26.5 reduce-scatter.3
  234.4 25.7 reduce-scatter.5
  263.9 69.9 reduce-scatter.7
